TPU v7x, 1024 devices: a whole 4x8x16 slice. The times are simulated.
1024 devices in a mesh: cuts: 4 (over x_lo, core), dp: 16 (over y, x_hi), tensor: 16 (over z).
Axes of the slice: x: 4 (x_hi: 2, x_lo: 2; x = x_hi * 2 + x_lo), y: 8, z: 16, core: 2. Of those that a mesh axis runs over, the one named last changes fastest.
Arguments:
- grad_out: bfloat16 [65536, 4096], P(('cuts', 'dp')), may hold values from -16 to 16
- attn_out: bfloat16 [65536, 4096], P(('cuts', 'dp'), 'tensor'), may hold values from -6 to 6
Outputs:
- grad_weight: float32 [4096, 4096], P(('cuts', 'dp'), 'tensor')
All inputs are finite; a program needn't handle non-finite values.
Results may differ from a plain program's by a relative error of at most 0.0003.
Values sent between devices are 32-bit elements; how exact they have to be, the bound alone decides.
No kernel may reach another device: no remote copies, remote signals or barrier semaphores. Data moves between devices by JAX's collectives and lax.ppermute only.
A program may use at most 32 MiB of HBM per device.

v0:
```python
import functools
import math

import jax
import jax.numpy as jnp
from jax import lax
from jax.experimental import pallas as pl
from jax.experimental.pallas import tpu as pltpu
from jax.sharding import Mesh, PartitionSpec as P


X, Y = 4, 8
COPIES = 2


def place(g):
    return (g & 1) * 2 + (g >> 5), (g >> 1) & 7, (g >> 4) & 1


def position(x, y, core):
    return (((x % 2) * 2 + core) * Y + y) * 2 + x // 2


def colour(x, y, core):
    return (x * (1 - 2 * core) + y * 2) & 3


def near(value, apart):
    dx, dy = {1: (1, 0), 2: (0, 1), 3: (-1, 0)}[apart]
    pairs = []
    for g in range(2 * X * Y):
        x, y, core = place(g)
        to = (x + dx * (1 - 2 * core)) % X, (y + dy * (1 - 2 * core)) % Y
        assert (colour(*to, core) - colour(x, y, core)) % 4 == apart
        pairs.append((g, position(*to, core)))
    return lax.ppermute(value, "g", pairs)


def far(value):
    groups = [[0] * 8 for _ in range(8)]
    for g in range(2 * X * Y):
        x, y, core = place(g)
        groups[core * 4 + colour(x, y, core)][y] = g
    return lax.all_to_all(value, "g", 0, 0, axis_index_groups=groups, tiled=True)


def half_kernel(other, grad_hbm, attn_hbm, out_ref, grad, attn, grad_sems, attn_sems):
    x, y, core = place(lax.axis_index("g"))
    core = core ^ other
    mine = colour(x, y, core)
    tokens, run = grad.shape[1:]
    cut = tokens // COPIES
    copies = {}
    for x_low in range(2):
        columns = pl.ds(pl.multiple_of((x_low * 2 + core) * run, run), run)
        for part in range(COPIES):
            rows = pl.ds(part * cut, cut)
            if x_low == 0:
                copies["attn", part] = pltpu.make_async_copy(
                    attn_hbm.at[rows, :], attn.at[rows, :], attn_sems.at[part]
                )
                copies["attn", part].start()
            copies[x_low, part] = pltpu.make_async_copy(
                grad_hbm.at[rows, columns], grad.at[x_low, rows, :], grad_sems.at[x_low, part]
            )
            copies[x_low, part].start()
    for x_low, parts in ((0, (0,)), (0, (1,)), (1, (0, 1))):
        for part in parts:
            if x_low == 0:
                copies["attn", part].wait()
            copies[x_low, part].wait()
        rows = slice(parts[0] * cut, (parts[-1] + 1) * cut)
        for k in range(Y):
            block = lax.dot_general(
                grad[x_low, rows, k * 128 : (k + 1) * 128],
                attn[rows, :],
                (((0,), (0,)), ((), ())),
                preferred_element_type=jnp.float32,
            )
            for x_high in range(2):
                x = x_high * 2 + x_low
                at = ((colour(x, k, core) - mine) & 3) * 8 + k
                term = block[x_high * 64 : (x_high + 1) * 64, :]
                out_ref[at] = out_ref[at] + term if parts == (1,) else term


def half(grad_out, attn_out, other):
    tokens, columns = attn_out.shape
    run = grad_out.shape[1] // 4
    return pl.pallas_call(
        functools.partial(half_kernel, other),
        out_shape=jax.ShapeDtypeStruct((X * Y, run // 16, columns), jnp.float32),
        in_specs=[pl.BlockSpec(memory_space=pltpu.HBM)] * 2,
        out_specs=pl.BlockSpec(memory_space=pltpu.VMEM),
        scratch_shapes=[
            pltpu.VMEM((2, tokens, run), jnp.bfloat16),
            pltpu.VMEM((tokens, columns), jnp.bfloat16),
            pltpu.SemaphoreType.DMA((2, COPIES)),
            pltpu.SemaphoreType.DMA((COPIES,)),
        ],
        compiler_params=pltpu.CompilerParams(vmem_limit_bytes=16 << 20),
        cost_estimate=pl.CostEstimate(
            flops=4 * tokens * run * columns,
            bytes_accessed=4 * tokens * run + 2 * tokens * columns + 8 * run * columns,
            transcendentals=0,
        ),
    )(grad_out, attn_out)


def body(grad_out, attn_out):
    factor = 1.0 / math.sqrt(float(grad_out.shape[0] * lax.axis_size("g")))
    grad_out, attn_out = (pltpu.with_memory_space_constraint(v, pltpu.HBM) for v in (grad_out, attn_out))
    theirs = half(grad_out, attn_out, 1)
    got = lax.ppermute(theirs, "g", [(s, s ^ 16) for s in range(2 * X * Y)])
    mine = half(grad_out, attn_out, 0)
    came = []
    for apart in range(1, 4):
        at = slice(apart * 8, apart * 8 + 8)
        came.append(near(mine[at] + got[at], apart))
    total = (mine[:8] + got[:8]) + came[0] + came[1] + came[2]
    terms = far(total)
    total = terms[0]
    for at in range(1, terms.shape[0]):
        total = total + terms[at]
    return total * factor


def solution(mesh):
    cuts, dp, tensor = mesh.devices.shape
    flat = Mesh(mesh.devices.reshape(cuts * dp, tensor), ("g", "z"))
    placed = (P("g", None), P("g", "z"))
    return jax.shard_map(body, mesh=flat, in_specs=placed, out_specs=P("g", "z"), check_vma=False)
```

profile of v0, /device:TPU:12, one launch (start us, length us, event | category | flops | bytes accessed | tf_op | source)
XLA Modules:
  0.0 60.5 jit_solution(13198760757554250899)
XLA Ops:
  0.0 3.4 %shard_map.29 = f32[32,64,256]{2,1,0:T(8,128)S(1)} custom-call(bf16[1024,4096]{1,0:T(8,128)(2,1)} %grad_hbm.3, bf16[1024,256]{1,0:T(8,128)(2,1)} %attn_hbm.3), custom_call_target="tpu_custom_call" | custom-call | flops 1073741824 | bytes 6815744 | tf_op jit(solution)/shard_map/pallas_call | solution.py:90
  3.4 1.9 %collective-permute-start = (f32[32,64,256]{2,1,0:T(8,128)S(1)}, f32[32,64,256]{2,1,0:T(8,128)S(1)}, u32[]{:S(2)}, u32[]{:S(2)}) collective-permute-start(f32[32,64,256]{2,1,0:T(8,128)S(1)} %shard_map.29), channel_id=1, source_target_pairs={{0,256},{16,272},{32,288},{48,304},{64,320},{80,336},{96,352},{112... | collective-permute-start | bytes 6291464 | tf_op jit(solution)/shard_map/ppermute | solution.py:114
  5.4 3.4 %shard_map.28 = f32[32,64,256]{2,1,0:T(8,128)S(1)} custom-call(bf16[1024,4096]{1,0:T(8,128)(2,1)} %grad_hbm.3, bf16[1024,256]{1,0:T(8,128)(2,1)} %attn_hbm.3), custom_call_target="tpu_custom_call" | custom-call | flops 1073741824 | bytes 6815744 | tf_op jit(solution)/shard_map/pallas_call | solution.py:90
  8.8 0.7 %collective-permute-done = f32[32,64,256]{2,1,0:T(8,128)S(1)} collective-permute-done((f32[32,64,256]{2,1,0:T(8,128)S(1)}, f32[32,64,256]{2,1,0:T(8,128)S(1)}, u32[]{:S(2)}, u32[]{:S(2)}) %collective-permute-start) | collective-permute-done | bytes 2097184 | tf_op jit(solution)/shard_map/ppermute | solution.py:114
  9.5 0.3 slice_add_fusion.2
  9.7 3.1 %collective-permute-start.1 = (f32[8,64,256]{2,1,0:T(8,128)S(1)}, f32[8,64,256]{2,1,0:T(8,128)S(1)}, u32[]{:S(2)}, u32[]{:S(2)}) collective-permute-start(f32[8,64,256]{2,1,0:T(8,128)S(1)} %get-tuple-element.5), channel_id=1, source_target_pairs={{0,512},{16,528},{32,544},{48,560},{64,576},{80,592},{96,608},{112... | collective-permute-start | bytes 1572872 | tf_op jit(solution)/shard_map/ppermute | solution.py:36
  12.9 2.7 %collective-permute-start.3 = (f32[8,64,256]{2,1,0:T(8,128)S(1)}, f32[8,64,256]{2,1,0:T(8,128)S(1)}, u32[]{:S(2)}, u32[]{:S(2)}) collective-permute-start(f32[8,64,256]{2,1,0:T(8,128)S(1)} %get-tuple-element.6), channel_id=1, source_target_pairs={{0,528},{16,512},{32,560},{48,544},{64,592},{80,576},{96,624},{112... | collective-permute-start | bytes 1572872 | tf_op jit(solution)/shard_map/ppermute | solution.py:36
  15.6 3.5 %collective-permute-start.2 = (f32[8,64,256]{2,1,0:T(8,128)S(1)}, f32[8,64,256]{2,1,0:T(8,128)S(1)}, u32[]{:S(2)}, u32[]{:S(2)}) collective-permute-start(f32[8,64,256]{2,1,0:T(8,128)S(1)} %get-tuple-element.7), channel_id=1, source_target_pairs={{0,32},{16,48},{32,64},{48,80},{64,96},{80,112},{96,128},{112,144}... | collective-permute-start | bytes 1572872 | tf_op jit(solution)/shard_map/ppermute | solution.py:36
  19.1 6.0 %collective-permute-done.1 = f32[8,64,256]{2,1,0:T(8,128)S(1)} collective-permute-done((f32[8,64,256]{2,1,0:T(8,128)S(1)}, f32[8,64,256]{2,1,0:T(8,128)S(1)}, u32[]{:S(2)}, u32[]{:S(2)}) %collective-permute-start.1) | collective-permute-done | bytes 524320 | tf_op jit(solution)/shard_map/ppermute | solution.py:36
  25.1 0.5 collective-permute-done.3
  25.6 1.1 %collective-permute-done.2 = f32[8,64,256]{2,1,0:T(8,128)S(1)} collective-permute-done((f32[8,64,256]{2,1,0:T(8,128)S(1)}, f32[8,64,256]{2,1,0:T(8,128)S(1)}, u32[]{:S(2)}, u32[]{:S(2)}) %collective-permute-start.2) | collective-permute-done | bytes 524320 | tf_op jit(solution)/shard_map/ppermute | solution.py:36
  26.7 0.2 fusion.2
  26.9 33.0 %all_to_all.5 = f32[8,64,256]{2,1,0:T(8,128)S(1)} all-to-all(f32[8,64,256]{2,1,0:T(8,128)S(1)} %fusion.2), channel_id=1, replica_groups={{0,48,64,112,128,176,192,240},{512,560,576,624,640,688,704,752},{16,32,..., dimensions={0} | all-to-all | bytes 1048576 | tf_op jit(solution)/shard_map/all_to_all | solution.py:44
  59.8 0.7 %fusion.4 = f32[64,256]{1,0:T(8,128)} fusion(f32[8,64,256]{2,1,0:T(8,128)S(1)} %all_to_all.5), kind=kLoop, calls=%fused_computation.9 | loop fusion | flops 131072 | bytes 589824 | tf_op jit(solution)/shard_map/mul | solution.py:125
Async XLA Ops:
  3.4 6.1 %collective-permute-start = (f32[32,64,256]{2,1,0:T(8,128)S(1)}, f32[32,64,256]{2,1,0:T(8,128)S(1)}, u32[]{:S(2)}, u32[]{:S(2)}) collective-permute-start(f32[32,64,256]{2,1,0:T(8,128)S(1)} %shard_map.29), channel_id=1, source_target_pairs={{0,256},{16,272},{32,288},{48,304},{64,320},{80,336},{96,352},{112... | collective-permute-start | bytes 6291464 | tf_op jit(solution)/shard_map/ppermute | solution.py:114
  9.7 15.3 %collective-permute-start.1 = (f32[8,64,256]{2,1,0:T(8,128)S(1)}, f32[8,64,256]{2,1,0:T(8,128)S(1)}, u32[]{:S(2)}, u32[]{:S(2)}) collective-permute-start(f32[8,64,256]{2,1,0:T(8,128)S(1)} %get-tuple-element.5), channel_id=1, source_target_pairs={{0,512},{16,528},{32,544},{48,560},{64,576},{80,592},{96,608},{112... | collective-permute-start | bytes 1572872 | tf_op jit(solution)/shard_map/ppermute | solution.py:36
  12.9 12.7 %collective-permute-start.3 = (f32[8,64,256]{2,1,0:T(8,128)S(1)}, f32[8,64,256]{2,1,0:T(8,128)S(1)}, u32[]{:S(2)}, u32[]{:S(2)}) collective-permute-start(f32[8,64,256]{2,1,0:T(8,128)S(1)} %get-tuple-element.6), channel_id=1, source_target_pairs={{0,528},{16,512},{32,560},{48,544},{64,592},{80,576},{96,624},{112... | collective-permute-start | bytes 1572872 | tf_op jit(solution)/shard_map/ppermute | solution.py:36
  15.6 11.1 %collective-permute-start.2 = (f32[8,64,256]{2,1,0:T(8,128)S(1)}, f32[8,64,256]{2,1,0:T(8,128)S(1)}, u32[]{:S(2)}, u32[]{:S(2)}) collective-permute-start(f32[8,64,256]{2,1,0:T(8,128)S(1)} %get-tuple-element.7), channel_id=1, source_target_pairs={{0,32},{16,48},{32,64},{48,80},{64,96},{80,112},{96,128},{112,144}... | collective-permute-start | bytes 1572872 | tf_op jit(solution)/shard_map/ppermute | solution.py:36
where the time goes:
time: 60.7 us; the launch traced here: 60.5 us
  blocking collectives  33 us (54%)
  starting transfers between devices  11.3 us (19%)
  waiting for transfers between devices  8.27 us (14%)
  Pallas kernels  6.85 us (11%)
  other arithmetic  1.1 us (2%)
    all_to_all x1, blocking collectives, far(): lax.all_to_all(value, 'g', 0, 0, axis_index_groups=groups, tiled=True)  33 us
    ppermute x3, starting transfers between devices, near(): return lax.ppermute(value, 'g', pairs)  9.33 us
    ppermute x3, waiting for transfers between devices, near(): return lax.ppermute(value, 'g', pairs)  7.58 us
    pallas_call x2, Pallas kernels, half(): pl.pallas_call(functools.partial(half_kernel, other), out_shape=jax.Shape...  6.85 us
    ppermute x1, starting transfers between devices, body(): got = lax.ppermute(theirs, 'g', [(s, s ^ 16) for s in range(2 * X * Y)])  1.92 us
  transfers between devices with their start and end apart: 4, of which 4 were waited for; matrix products, arithmetic and copies ran while one was open for 0% of the time, Pallas kernels for 6%

commit v1 on v0

v1 whole, which is shorter than its diff:
```python
import functools
import math

import jax
import jax.numpy as jnp
from jax import lax
from jax.experimental import pallas as pl
from jax.experimental.pallas import tpu as pltpu
from jax.sharding import Mesh, PartitionSpec as P


X, Y = 4, 8
COPIES = 2


def place(g):
    return (g & 1) * 2 + (g >> 5), (g >> 1) & 7, (g >> 4) & 1


def position(x, y, core):
    return (((x % 2) * 2 + core) * Y + y) * 2 + x // 2


def colour(x, y, core):
    return (x * (1 - 2 * core) + y * 2) & 3


def near(value, apart):
    dx, dy = {1: (1, 0), 2: (0, 1), 3: (-1, 0)}[apart]
    pairs = []
    for g in range(2 * X * Y):
        x, y, core = place(g)
        to = (x + dx * (1 - 2 * core)) % X, (y + dy * (1 - 2 * core)) % Y
        assert (colour(*to, core) - colour(x, y, core)) % 4 == apart
        pairs.append((g, position(*to, core)))
    return lax.ppermute(value, "g", pairs)


def far(value):
    groups = [[0] * 8 for _ in range(8)]
    for g in range(2 * X * Y):
        x, y, core = place(g)
        groups[core * 4 + colour(x, y, core)][y] = g
    return lax.all_to_all(value, "g", 0, 0, axis_index_groups=groups, tiled=True)


def where(other, apart):
    x, y, core = place(lax.axis_index("g"))
    core = core ^ other
    x_low = (x + apart) & 1
    return x_low * 2 + core, core, x_low, colour(x, y, core)


def multiply(other, apart, rows, grad, first, attn, out_ref, add):
    _, core, x_low, mine = where(other, apart)
    for k in range(Y):
        block = lax.dot_general(
            grad[rows, pl.ds(first + k * 128, 128)],
            attn[rows, :],
            (((0,), (0,)), ((), ())),
            preferred_element_type=jnp.float32,
        )
        for x_high in range(2):
            far_off = (colour(x_high * 2 + x_low, k, core) - mine) & 3
            at = (far_off >> 1) * 8 + k
            term = block[x_high * 64 : (x_high + 1) * 64, :]
            out_ref[at] = out_ref[at] + term if add else term


def first_kernel(other, apart, grad_hbm, attn_hbm, out_ref, grad, attn, sems):
    tokens, run = grad.shape
    columns = pl.ds(pl.multiple_of(where(other, apart)[0] * run, run), run)
    copies = []
    for part in range(COPIES):
        rows = pl.ds(part * (tokens // COPIES), tokens // COPIES)
        for at, (source, target) in enumerate(
            ((attn_hbm.at[rows, :], attn.at[rows, :]), (grad_hbm.at[rows, columns], grad.at[rows, :]))
        ):
            copies.append(pltpu.make_async_copy(source, target, sems.at[part, at]))
            copies[-1].start()
    for part in range(COPIES):
        copies[2 * part].wait()
        copies[2 * part + 1].wait()
        rows = slice(part * (tokens // COPIES), (part + 1) * (tokens // COPIES))
        multiply(other, apart, rows, grad, 0, attn, out_ref, part > 0)


def later_kernel(other, apart, grad_ref, attn_ref, out_ref):
    run = grad_ref.shape[1] // 4
    first = pl.multiple_of(where(other, apart)[0] * run, run)
    multiply(other, apart, slice(None), grad_ref, first, attn_ref, out_ref, False)


def term(grad_out, attn_out, other, apart, first):
    tokens, columns = attn_out.shape
    run = grad_out.shape[1] // 4
    scratch = [
        pltpu.VMEM((tokens, run), jnp.bfloat16),
        pltpu.VMEM((tokens, columns), jnp.bfloat16),
        pltpu.SemaphoreType.DMA((COPIES, 2)),
    ]
    return pl.pallas_call(
        functools.partial(first_kernel if first else later_kernel, other, apart),
        out_shape=jax.ShapeDtypeStruct((X * Y // 2, run // 16, columns), jnp.float32),
        in_specs=[pl.BlockSpec(memory_space=pltpu.HBM if first else pltpu.VMEM)] * 2,
        out_specs=pl.BlockSpec(memory_space=pltpu.VMEM),
        scratch_shapes=scratch if first else [],
        compiler_params=pltpu.CompilerParams(vmem_limit_bytes=8 << 20),
        cost_estimate=pl.CostEstimate(
            flops=2 * tokens * run * columns,
            bytes_accessed=2 * tokens * run + 2 * tokens * columns + 4 * run * columns,
            transcendentals=0,
        ),
    )(grad_out, attn_out)


def body(grad_out, attn_out):
    factor = 1.0 / math.sqrt(float(grad_out.shape[0] * lax.axis_size("g")))
    in_hbm = [pltpu.with_memory_space_constraint(v, pltpu.HBM) for v in (grad_out, attn_out)]
    swap = [(s, s ^ 16) for s in range(2 * X * Y)]
    got_odd = lax.ppermute(term(*in_hbm, 1, 1, True), "g", swap)
    got_even = lax.ppermute(term(grad_out, attn_out, 1, 0, False), "g", swap)
    mine_odd = term(grad_out, attn_out, 0, 1, False)
    one = near(mine_odd[:8] + got_odd[:8], 1)
    three = near(mine_odd[8:] + got_odd[8:], 3)
    mine_even = term(grad_out, attn_out, 0, 0, False)
    two = near(mine_even[8:] + got_even[8:], 2)
    total = (mine_even[:8] + got_even[:8]) + one + three + two
    terms = far(total)
    total = terms[0]
    for at in range(1, terms.shape[0]):
        total = total + terms[at]
    return total * factor


def solution(mesh):
    cuts, dp, tensor = mesh.devices.shape
    flat = Mesh(mesh.devices.reshape(cuts * dp, tensor), ("g", "z"))
    placed = (P("g", None), P("g", "z"))
    return jax.shard_map(body, mesh=flat, in_specs=placed, out_specs=P("g", "z"), check_vma=False)
```

time: 60.7 us -> 60.9 us (level)
  starting transfers between devices: 11.3 us -> 13.8 us
  Pallas kernels: 6.85 us -> 5.21 us
  waiting for transfers between devices: 8.27 us -> 7.59 us
    ppermute x1 -> x2, starting transfers between devices: 1.92 us -> 4.46 us  [the longest x1 2.4 us: body(): got_even = lax.ppermute(term(grad_out, attn_out, 1, 0, False), 'g', swap)]
    pallas_call x2 -> x4, Pallas kernels: 6.85 us -> 5.21 us  [term(): pl.pallas_call(functools.partial(first_kernel if first else later_kernel,...]
    ppermute x1 -> x2, waiting for transfers between devices: 0.69 us -> 0.01 us  [the longest x1 0.01 us: body(): got_odd = lax.ppermute(term(*in_hbm, 1, 1, True), 'g', swap)]
  transfers between devices with their start and end apart: 4 -> 5, of which waited for: 4 -> 3; matrix products, arithmetic and copies ran while one was open for 0% -> 0% of each run, Pallas kernels for 6% -> 4%
where the time goes in v1:
time: 60.9 us; the launch traced here: 60.6 us
  blocking collectives  32.8 us (54%)
  starting transfers between devices  13.8 us (23%)
  waiting for transfers between devices  7.59 us (12%)
  Pallas kernels  5.21 us (9%)
  other arithmetic  1.05 us (2%)
    all_to_all x1, blocking collectives, far(): lax.all_to_all(value, 'g', 0, 0, axis_index_groups=groups, tiled=True)  32.8 us
    ppermute x3, starting transfers between devices, near(): return lax.ppermute(value, 'g', pairs)  9.33 us
    ppermute x3, waiting for transfers between devices, near(): return lax.ppermute(value, 'g', pairs)  7.58 us
    pallas_call x4, Pallas kernels, term(): pl.pallas_call(functools.partial(first_kernel if first else later_kernel,...  5.21 us
    ppermute x1, starting transfers between devices, body(): got_even = lax.ppermute(term(grad_out, attn_out, 1, 0, False), 'g', swap)  2.4 us
    ppermute x1, starting transfers between devices, body(): got_odd = lax.ppermute(term(*in_hbm, 1, 1, True), 'g', swap)  2.05 us
  transfers between devices with their start and end apart: 5, of which 3 were waited for; matrix products, arithmetic and copies ran while one was open for 0% of the time, Pallas kernels for 4%

profile of v1, /device:TPU:12, one launch (start us, length us, event | category | flops | bytes accessed | tf_op | source)
XLA Modules:
  0.0 60.6 jit_solution(17187058916800823618)
XLA Ops:
  0.0 0.0 copy-start.1
  0.0 0.0 copy-start
  0.0 2.6 %shard_map.31 = f32[16,64,256]{2,1,0:T(8,128)S(1)} custom-call(bf16[1024,4096]{1,0:T(8,128)(2,1)} %grad_hbm.1, bf16[1024,256]{1,0:T(8,128)(2,1)} %attn_hbm.1), custom_call_target="tpu_custom_call" | custom-call | flops 536870912 | bytes 3670016 | tf_op jit(solution)/shard_map/pallas_call | solution.py:102
  2.6 2.1 %collective-permute-start.1 = (f32[16,64,256]{2,1,0:T(8,128)S(1)}, f32[16,64,256]{2,1,0:T(8,128)S(1)}, u32[]{:S(2)}, u32[]{:S(2)}) collective-permute-start(f32[16,64,256]{2,1,0:T(8,128)S(1)} %shard_map.31), channel_id=1, source_target_pairs={{0,256},{16,272},{32,288},{48,304},{64,320},{80,336},{96,352},{112... | collective-permute-start | bytes 3145736 | tf_op jit(solution)/shard_map/ppermute | solution.py:121
  4.7 0.0 copy-done.1
  4.7 0.0 copy-done
  4.7 0.9 %shard_map.29 = f32[16,64,256]{2,1,0:T(8,128)S(1)} custom-call(bf16[1024,4096]{1,0:T(8,128)(2,1)S(1)} %copy-done, bf16[1024,256]{1,0:T(8,128)(2,1)S(1)} %copy-done.1), custom_call_target="tpu_custom_call" | custom-call | flops 536870912 | bytes 3670016 | tf_op jit(solution)/shard_map/pallas_call | solution.py:102
  5.6 2.4 %collective-permute-start = (f32[16,64,256]{2,1,0:T(8,128)S(1)}, f32[16,64,256]{2,1,0:T(8,128)S(1)}, u32[]{:S(2)}, u32[]{:S(2)}) collective-permute-start(f32[16,64,256]{2,1,0:T(8,128)S(1)} %shard_map.29), channel_id=1, source_target_pairs={{0,256},{16,272},{32,288},{48,304},{64,320},{80,336},{96,352},{112... | collective-permute-start | bytes 3145736 | tf_op jit(solution)/shard_map/ppermute | solution.py:122
  8.0 0.9 %shard_map.28 = f32[16,64,256]{2,1,0:T(8,128)S(1)} custom-call(bf16[1024,4096]{1,0:T(8,128)(2,1)S(1)} %copy-done, bf16[1024,256]{1,0:T(8,128)(2,1)S(1)} %copy-done.1), custom_call_target="tpu_custom_call" | custom-call | flops 536870912 | bytes 3670016 | tf_op jit(solution)/shard_map/pallas_call | solution.py:102
  8.9 0.9 %shard_map.30 = f32[16,64,256]{2,1,0:T(8,128)S(1)} custom-call(bf16[1024,4096]{1,0:T(8,128)(2,1)S(1)} %copy-done, bf16[1024,256]{1,0:T(8,128)(2,1)S(1)} %copy-done.1), custom_call_target="tpu_custom_call" | custom-call | flops 536870912 | bytes 3670016 | tf_op jit(solution)/shard_map/pallas_call | solution.py:102
  9.7 0.0 collective-permute-done.1
  9.7 0.1 slice_add_fusion.2
  9.9 3.1 %collective-permute-start.2 = (f32[8,64,256]{2,1,0:T(8,128)S(1)}, f32[8,64,256]{2,1,0:T(8,128)S(1)}, u32[]{:S(2)}, u32[]{:S(2)}) collective-permute-start(f32[8,64,256]{2,1,0:T(8,128)S(1)} %get-tuple-element.5), channel_id=1, source_target_pairs={{0,512},{16,528},{32,544},{48,560},{64,576},{80,592},{96,608},{112... | collective-permute-start | bytes 1572872 | tf_op jit(solution)/shard_map/ppermute | solution.py:36
  13.0 2.7 %collective-permute-start.3 = (f32[8,64,256]{2,1,0:T(8,128)S(1)}, f32[8,64,256]{2,1,0:T(8,128)S(1)}, u32[]{:S(2)}, u32[]{:S(2)}) collective-permute-start(f32[8,64,256]{2,1,0:T(8,128)S(1)} %get-tuple-element.6), channel_id=1, source_target_pairs={{0,528},{16,512},{32,560},{48,544},{64,592},{80,576},{96,624},{112... | collective-permute-start | bytes 1572872 | tf_op jit(solution)/shard_map/ppermute | solution.py:36
  15.8 0.0 collective-permute-done
  15.8 0.1 slice_add_fusion
  15.8 3.5 %collective-permute-start.4 = (f32[8,64,256]{2,1,0:T(8,128)S(1)}, f32[8,64,256]{2,1,0:T(8,128)S(1)}, u32[]{:S(2)}, u32[]{:S(2)}) collective-permute-start(f32[8,64,256]{2,1,0:T(8,128)S(1)} %slice_add_fusion), channel_id=1, source_target_pairs={{0,32},{16,48},{32,64},{48,80},{64,96},{80,112},{96,128},{112,144}... | collective-permute-start | bytes 1572872 | tf_op jit(solution)/shard_map/ppermute | solution.py:36
  19.3 6.0 %collective-permute-done.2 = f32[8,64,256]{2,1,0:T(8,128)S(1)} collective-permute-done((f32[8,64,256]{2,1,0:T(8,128)S(1)}, f32[8,64,256]{2,1,0:T(8,128)S(1)}, u32[]{:S(2)}, u32[]{:S(2)}) %collective-permute-start.2) | collective-permute-done | bytes 524320 | tf_op jit(solution)/shard_map/ppermute | solution.py:36
  25.4 0.3 collective-permute-done.3
  25.6 1.3 %collective-permute-done.4 = f32[8,64,256]{2,1,0:T(8,128)S(1)} collective-permute-done((f32[8,64,256]{2,1,0:T(8,128)S(1)}, f32[8,64,256]{2,1,0:T(8,128)S(1)}, u32[]{:S(2)}, u32[]{:S(2)}) %collective-permute-start.4) | collective-permute-done | bytes 524320 | tf_op jit(solution)/shard_map/ppermute | solution.py:36
  26.9 0.2 fusion.2
  27.1 32.8 %all_to_all.5 = f32[8,64,256]{2,1,0:T(8,128)S(1)} all-to-all(f32[8,64,256]{2,1,0:T(8,128)S(1)} %fusion.2), channel_id=1, replica_groups={{0,48,64,112,128,176,192,240},{512,560,576,624,640,688,704,752},{16,32,..., dimensions={0} | all-to-all | bytes 1048576 | tf_op jit(solution)/shard_map/all_to_all | solution.py:44
  59.9 0.7 %fusion.4 = f32[64,256]{1,0:T(8,128)} fusion(f32[8,64,256]{2,1,0:T(8,128)S(1)} %all_to_all.5), kind=kLoop, calls=%fused_computation.9 | loop fusion | flops 131072 | bytes 589824 | tf_op jit(solution)/shard_map/mul | solution.py:133
Async XLA Ops:
  0.0 4.7 %copy-start.1 = (bf16[1024,256]{1,0:T(8,128)(2,1)S(1)}, bf16[1024,256]{1,0:T(8,128)(2,1)}, u32[]{:S(2)}) copy-start(bf16[1024,256]{1,0:T(8,128)(2,1)} %attn_hbm.1) | copy-start | bytes 1572868
  0.0 4.7 %copy-start = (bf16[1024,4096]{1,0:T(8,128)(2,1)S(1)}, bf16[1024,4096]{1,0:T(8,128)(2,1)}, u32[]{:S(2)}) copy-start(bf16[1024,4096]{1,0:T(8,128)(2,1)} %grad_hbm.1) | copy-start | bytes 25165828
  2.6 7.1 %collective-permute-start.1 = (f32[16,64,256]{2,1,0:T(8,128)S(1)}, f32[16,64,256]{2,1,0:T(8,128)S(1)}, u32[]{:S(2)}, u32[]{:S(2)}) collective-permute-start(f32[16,64,256]{2,1,0:T(8,128)S(1)} %shard_map.31), channel_id=1, source_target_pairs={{0,256},{16,272},{32,288},{48,304},{64,320},{80,336},{96,352},{112... | collective-permute-start | bytes 3145736 | tf_op jit(solution)/shard_map/ppermute | solution.py:121
  5.6 10.2 %collective-permute-start = (f32[16,64,256]{2,1,0:T(8,128)S(1)}, f32[16,64,256]{2,1,0:T(8,128)S(1)}, u32[]{:S(2)}, u32[]{:S(2)}) collective-permute-start(f32[16,64,256]{2,1,0:T(8,128)S(1)} %shard_map.29), channel_id=1, source_target_pairs={{0,256},{16,272},{32,288},{48,304},{64,320},{80,336},{96,352},{112... | collective-permute-start | bytes 3145736 | tf_op jit(solution)/shard_map/ppermute | solution.py:122
  9.9 15.5 %collective-permute-start.2 = (f32[8,64,256]{2,1,0:T(8,128)S(1)}, f32[8,64,256]{2,1,0:T(8,128)S(1)}, u32[]{:S(2)}, u32[]{:S(2)}) collective-permute-start(f32[8,64,256]{2,1,0:T(8,128)S(1)} %get-tuple-element.5), channel_id=1, source_target_pairs={{0,512},{16,528},{32,544},{48,560},{64,576},{80,592},{96,608},{112... | collective-permute-start | bytes 1572872 | tf_op jit(solution)/shard_map/ppermute | solution.py:36
  13.0 12.6 %collective-permute-start.3 = (f32[8,64,256]{2,1,0:T(8,128)S(1)}, f32[8,64,256]{2,1,0:T(8,128)S(1)}, u32[]{:S(2)}, u32[]{:S(2)}) collective-permute-start(f32[8,64,256]{2,1,0:T(8,128)S(1)} %get-tuple-element.6), channel_id=1, source_target_pairs={{0,528},{16,512},{32,560},{48,544},{64,592},{80,576},{96,624},{112... | collective-permute-start | bytes 1572872 | tf_op jit(solution)/shard_map/ppermute | solution.py:36
  15.8 11.1 %collective-permute-start.4 = (f32[8,64,256]{2,1,0:T(8,128)S(1)}, f32[8,64,256]{2,1,0:T(8,128)S(1)}, u32[]{:S(2)}, u32[]{:S(2)}) collective-permute-start(f32[8,64,256]{2,1,0:T(8,128)S(1)} %slice_add_fusion), channel_id=1, source_target_pairs={{0,32},{16,48},{32,64},{48,80},{64,96},{80,112},{96,128},{112,144}... | collective-permute-start | bytes 1572872 | tf_op jit(solution)/shard_map/ppermute | solution.py:36
